TPU v7x, 256 devices: a whole 4x4x8 slice. The times are simulated.
256 devices in a mesh: mod: 2 (over core), seq: 8 (over z), tp: 16 (over x, y).
Axes of the slice: x: 4, y: 4, z: 8, core: 2. Of those that a mesh axis runs over, the one named last changes fastest.
Arguments:
- tokens: bfloat16 [8192, 4096], P(('mod', 'seq'), 'tp'), may hold values from -6 to 6
- modality: int32 [8192], replicated, may hold values from 0 to 1, as said below
- norm_gain: float32 [2, 4096], replicated, may hold values from 0.1 to 1.9
- input_weight: bfloat16 [2, 4096, 3, 4096], P('mod', None, None, 'tp'), may hold values from -0.09375 to 0.09375
- head_gain: float32 [2, 2, 128], replicated, may hold values from 1 to 2
- output_weight: bfloat16 [2, 4096, 4096], P('mod', 'tp'), may hold values from -0.125 to 0.125
Outputs:
- update: bfloat16 [8192, 4096], P(('mod', 'seq'), 'tp')
Inputs may be any that keep to these rules, and one draw needn't show every extreme that they name: Each value is constant over aligned spans of 64 tokens. Each token shard (the 512 tokens of one index of mod+seq) holds between 3 and 5 image spans, so at most 320 tokens of either modality. In every draw, for some index of seq both of its token shards hold 320 text tokens, and for another index of seq both hold 320 image tokens.
All inputs are finite; a program needn't handle non-finite values.
Results may differ from a plain program's by a relative error of at most 0.019.
Values may be sent and summed in bfloat16 or wider, within the bound.
A program may use at most 192 MiB of HBM per device.

v0:
```python
from functools import partial
import math
import jax
import jax.numpy as jnp
from jax import lax
from jax.sharding import PartitionSpec as P

HD = 128
CAP = 320
epsilon = 1e-05
sentinel = 1 << 30


def route_table(shard_ids, shard_index, slot_count):
    length = shard_ids.shape[0]
    order = jnp.argsort(shard_ids, stable=True)
    text_count = jnp.sum((shard_ids == 0).astype(jnp.int32))
    padded = jnp.concatenate([order, jnp.zeros((slot_count,), jnp.int32)])
    slot_index = jnp.arange(slot_count, dtype=jnp.int32)
    picked = jnp.stack(
        [padded[:slot_count], lax.dynamic_slice_in_dim(padded, text_count, slot_count)]
    )
    live = jnp.stack([slot_index < text_count, slot_index < length - text_count])
    place = shard_index * length + picked
    query_place = jnp.where(live, place, -1)
    key_place = jnp.where(live, place, sentinel)
    return (order, text_count, picked, live, query_place, key_place)


def select_rows(table, picked, live):
    return jnp.where(live[:, :, None], table[picked], jnp.zeros((), table.dtype))


def head_norm(part, gain):
    return part * lax.rsqrt(jnp.mean(part * part, axis=-1, keepdims=True) + epsilon) * gain


def body(tokens, modality, norm_gain, input_weight, head_gain, output_weight):
    length = tokens.shape[0]
    mod_count = lax.axis_size("mod")
    seq_count = lax.axis_size("seq")
    shards = mod_count * seq_count
    mine = lax.axis_index("mod")
    seq_index = lax.axis_index("seq")
    all_ids = modality.reshape(shards, length)
    own_index = mine * seq_count + seq_index
    own_ids = lax.dynamic_index_in_dim(all_ids, own_index, 0, keepdims=False)
    own_table = route_table(own_ids, own_index, CAP)
    order = own_table[0]
    text_count = own_table[1]
    picked = own_table[2]
    live = own_table[3]
    tables = jax.vmap(partial(route_table, slot_count=CAP))(
        all_ids, jnp.arange(shards, dtype=jnp.int32)
    )
    query_grid = tables[4].reshape(mod_count, seq_count, 2, CAP)
    own_query = lax.dynamic_index_in_dim(query_grid, seq_index, 1, keepdims=False)
    own_query = lax.dynamic_index_in_dim(own_query, mine, 1, keepdims=False).reshape(
        mod_count * CAP
    )
    key_grid = tables[5].reshape(mod_count, seq_count, 2, CAP)
    key_order = jnp.transpose(key_grid, (2, 1, 0, 3)).reshape(shards * mod_count * CAP)
    gathered = lax.all_gather(tokens, "tp", axis=1, tiled=True)
    arrived = lax.all_to_all(
        select_rows(gathered, picked, live), "mod", split_axis=0, concat_axis=0, tiled=True
    )
    rows_total = arrived.shape[0] * arrived.shape[1]
    width = arrived.shape[2]
    states = arrived.reshape(rows_total, width).astype(jnp.float32)
    gain = lax.dynamic_index_in_dim(norm_gain, mine, 0, keepdims=False)
    normed = (
        states * lax.rsqrt(jnp.mean(states * states, axis=1, keepdims=True) + epsilon) * gain
    ).astype(jnp.bfloat16)
    local_width = input_weight.shape[3]
    heads_here = local_width // HD
    projected = jnp.dot(
        normed, input_weight[0].reshape(width, 3 * local_width), preferred_element_type=jnp.float32
    )
    projected = projected.reshape(rows_total, 3, heads_here, HD)
    gains = lax.dynamic_index_in_dim(head_gain, mine, 0, keepdims=False)
    query_rows = head_norm(projected[:, 0], gains[0]).astype(jnp.bfloat16)
    key_rows = (
        head_norm(projected[:, 1], gains[1]).astype(jnp.bfloat16).reshape(rows_total, local_width)
    )
    value_rows = projected[:, 2].astype(jnp.bfloat16).reshape(rows_total, local_width)
    scale = 1.0 / math.sqrt(HD)
    key_piece = lax.all_gather(key_rows, ("mod", "seq"), axis=0, tiled=True)
    value_piece = lax.all_gather(value_rows, ("mod", "seq"), axis=0, tiled=True)
    count = key_piece.shape[0]
    scores = (
        jnp.einsum(
            "rhe,khe->hrk",
            query_rows,
            key_piece.reshape(count, heads_here, HD),
            preferred_element_type=jnp.float32,
        )
        * scale
    )
    weights = jnp.where(key_order[None, None, :] <= own_query[None, :, None], jnp.exp(scores), 0.0)
    totals = jnp.sum(weights, axis=2)
    rounded = weights.astype(jnp.bfloat16)
    weighted = jnp.einsum(
        "hrk,khe->rhe",
        rounded,
        value_piece.reshape(count, heads_here, HD),
        preferred_element_type=jnp.float32,
    )
    weighted, totals = (weighted, totals)
    totals = jnp.where(own_query[None, :] >= 0, totals, 1.0)
    attention = (
        (weighted / jnp.transpose(totals)[:, :, None])
        .astype(jnp.bfloat16)
        .reshape(rows_total, local_width)
    )
    head_terms = jnp.dot(attention, output_weight[0], preferred_element_type=jnp.float32)
    summed = lax.psum_scatter(
        head_terms.astype(jnp.bfloat16), "tp", scatter_dimension=1, tiled=True
    ).astype(jnp.float32)
    result = summed.astype(jnp.bfloat16).reshape(mod_count, CAP, summed.shape[1])
    returned = lax.all_to_all(result, "mod", split_axis=0, concat_axis=0, tiled=True)
    flat = returned.reshape(mod_count * CAP, summed.shape[1])
    inverse = jnp.zeros((length,), jnp.int32).at[order].set(jnp.arange(length, dtype=jnp.int32))
    slot = own_ids * CAP + inverse - own_ids * text_count
    return flat[slot]


def solution(mesh):
    in_specs = (
        P(("mod", "seq"), "tp"),
        P(),
        P(),
        P("mod", None, None, "tp"),
        P(),
        P("mod", "tp", None),
    )
    out_specs = P(("mod", "seq"), "tp")
    return jax.shard_map(body, mesh=mesh, in_specs=in_specs, out_specs=out_specs, check_vma=False)
```

profile of v0, /device:TPU:1, one launch (start us, length us, event | category | flops | bytes accessed | tf_op | source)
XLA Modules:
  0.0 324.6 jit_solution(6976612528921012147)
XLA Ops:
  8.1 1.4 reshape.304
  12.9 3.8 %sort.34 = (s32[512]{0:T(512)}, s32[512]{0:T(512)S(1)}) sort(s32[512]{0:T(512)S(1)} %bitcast.92, s32[512]{0:T(512)S(1)} %iota.35), dimensions={0}, to_apply=%region_1.2 | sort | flops 4608 | bytes 8192 | tf_op jit(solution)/shard_map/jit(argsort)/sort | solution.py:16
  18.8 8.8 %copy.12 = bf16[1,4096,3,256]{1,3,2,0:T(8,128)(2,1)} copy(bf16[1,4096,3,256]{3,1,2,0:T(8,128)(2,1)} %param.9) | data formatting | bytes 12582912 | tf_op args[3]
  27.7 48.4 %all-gather.4.cloned.1.call-done = bf16[512,4096]{1,0:T(8,128)(2,1)} async-done(((bf16[512,256]{1,0:T(8,128)(2,1)}), bf16[512,4096]{1,0:T(8,128)(2,1)}) %all-gather.4.cloned.1.call-update) | async-done | bytes 4194320 | tf_op jit(solution)/shard_map/all_gather | solution.py:63
  76.1 14.3 %gather_fusion = bf16[640,4096]{1,0:T(8,128)(2,1)} fusion(bf16[512,4096]{1,0:T(8,128)(2,1)} %all-gather.4.cloned.1.call-done, s32[1024]{0:T(1024)S(1)} %pad_clamp_fusion.1), kind=kCustom, calls=%fused_computation | custom fusion | bytes 10488320 | tf_op jit(solution)/shard_map/gather | solution.py:31
  90.5 2.9 broadcast_select_fusion
  93.4 9.2 %all_to_all.10 = bf16[2,320,4096]{2,1,0:T(8,128)(2,1)S(1)} all-to-all(bf16[2,320,4096]{2,1,0:T(8,128)(2,1)S(1)} %broadcast_select_fusion), channel_id=1, replica_groups=mesh['mod'=2,'seq'=8,'tp'=16] {'mod'}, dimensions={0} | all-to-all | bytes 10485760 | tf_op jit(solution)/shard_map/all_to_all | solution.py:64
  103.7 2.1 fusion.7
  105.8 5.1 %fusion.29 = f32[640,3,2,128]{0,3,2,1:T(8,128)S(1)} fusion(bf16[640,4096,1,1]{1,0,3,2:T(8,128)(2,1)S(1)} %bitcast.85, bf16[3,2,128,4096]{3,2,1,0:T(8,128)(2,1)S(1)} %bitcast.84), kind=kOutput, calls=%fused_computation.75 | convolution fusion | flops 4026531840 | bytes 13500416 | tf_op jit(solution)/shard_map/dot_general | solution.py:76
  110.9 1.3 copy-done.1
  115.0 1.8 slice.59
  117.2 30.9 %while.1 = (s32[]{:T(128)}, s32[16,832]{1,0:T(8,128)S(1)}, s32[16,2]{0,1:T(2,128)S(1)}, s32[16,320]{1,0:T(8,128)S(1)}, s32[]{:T(128)}, /*index=5*/s32[]{:T(128)}) while((s32[]{:T(128)}, s32[16,832]{1,0:T(8,128)S(1)}, s32[16,2]{0,1:T(2,128)S(1)}, s32[16,320]{1,0:T(8,128)S(1)}, s32[]{:T(128)}, /*index=5*/s32[]{:T(128)}) %tuple.26), condition=%wide.while_cond, body=%wide.while_body.sunk | while | flops 2 | bytes 5233 | solution.py:21
  129.4 1.3 dynamic-slice.9
  139.0 1.3 dynamic-slice.9
  142.9 1.3 dynamic-slice.9
  148.4 6.8 %broadcast_compare_fusion = pred[640,10240]{1,0:T(8,128)(4,1)} fusion(s32[10240]{0:T(1024)S(1)} %le.22, s32[640]{0:T(1024)S(1)} %le.24), kind=kLoop, calls=%fused_computation.9 | loop fusion | flops 6553600 | bytes 6597120 | tf_op jit(solution)/shard_map/le | solution.py:99
  156.5 26.4 %fusion = (f32[2,640]{1,0:T(2,128)S(1)}, f32[2,640,10240]{2,1,0:T(8,128)}) fusion(pred[640,10240]{1,0:T(8,128)(4,1)} %broadcast_compare_fusion, bf16[10240,2,128]{0,2,1:T(8,128)(2,1)} %bitcast.95, f32[640,3,2,128]{0,3,2,1:T(8,128)} %copy-done.1, f32[128]{0:T(128)S(1)} %get-tuple-element.33, f32[640,2]{0,1:T(2,128)S(1)} %add_rsqrt_fusion.1), kind=kOutput, calls=%fused_computation.5 | convolution fusion | flops 3395255040 | bytes 64891392 | tf_op jit(solution)/shard_map/rhe,khe->hrk/dot_general | solution.py:91
  182.9 18.0 %all-gather.6.cloned.1.call-done = bf16[10240,256]{0,1:T(8,128)(2,1)} async-done(((bf16[640,256]{0,1:T(8,128)(2,1)}), bf16[10240,256]{0,1:T(8,128)(2,1)}) %all-gather.6.cloned.1.call-update) | async-done | bytes 5242896 | tf_op jit(solution)/shard_map/all_gather | solution.py:88
  200.9 22.6 %fusion.15 = bf16[640,2,128]{0,2,1:T(8,128)(2,1)S(1)} fusion(bf16[10240,2,128]{0,2,1:T(8,128)(2,1)} %bitcast.96, f32[2,640,10240]{2,1,0:T(8,128)} %get-tuple-element.36, pred[640,10240]{1,0:T(8,128)(4,1)} %broadcast_compare_fusion, f32[640,2]{0,1:T(2,128)S(1)} %select_bitcast_fusion.2), kind=kOutput, calls=%fused_computation.20 | convolution fusion | flops 3395092480 | bytes 64558080 | tf_op jit(solution)/shard_map/hrk,khe->rhe/dot_general | solution.py:102
  223.5 3.9 %convolution_convert_fusion = bf16[640,4096]{1,0:T(8,128)(2,1)} fusion(bf16[640,256]{0,1:T(8,128)(2,1)S(1)} %bitcast.87, bf16[1,256,4096]{2,1,0:T(8,128)(2,1)S(1)} %copy-done), kind=kOutput, calls=%fused_computation.15 | convolution fusion | flops 1344798720 | bytes 7667712 | tf_op jit(solution)/shard_map/dot_general | solution.py:115
  227.4 2.4 scatter_custom_fusion
  230.5 77.9 %reduce-scatter.2.cloned.1.call-done = bf16[640,256]{1,0:T(8,128)(2,1)} async-done(((bf16[640,4096]{1,0:T(8,128)(2,1)}), bf16[640,256]{1,0:T(8,128)(2,1)}) %reduce-scatter.2.cloned.1.call-update) | async-done | bytes 327696 | tf_op jit(solution)/shard_map/reduce_scatter | solution.py:116
  308.5 6.4 %all_to_all.11 = bf16[2,320,256]{2,1,0:T(8,128)(2,1)S(1)} all-to-all(bf16[2,320,256]{2,1,0:T(8,128)(2,1)} %bitcast.88), channel_id=1, replica_groups=mesh['mod'=2,'seq'=8,'tp'=16] {'mod'}, dimensions={0} | all-to-all | bytes 655360 | tf_op jit(solution)/shard_map/all_to_all | solution.py:120
  314.9 2.6 gather_fusion.1
  (131 shorter events, 36.8 us)
Async XLA Ops:
  7.4 216.1 %copy-start = (bf16[1,256,4096]{2,1,0:T(8,128)(2,1)S(1)}, bf16[1,256,4096]{2,1,0:T(8,128)(2,1)}, u32[]{:S(2)}) copy-start(bf16[1,256,4096]{2,1,0:T(8,128)(2,1)} %param.11) | copy-start | bytes 6291460
  7.4 68.8 %all-gather.4.cloned.1.call-start = ((), (), s32[]{:S(2)}) async-start(), calls=%async_computation.3 | async-start | bytes 4456448 | tf_op jit(solution)/shard_map/all_gather | solution.py:63
  8.1 105.4 %sort.37.cloned.1.call-start = ((), (), s32[]{:S(2)}) async-start(), calls=%async_computation.7 | async-start | bytes 196640 | tf_op jit(solution)/shard_map/vmap(jit(argsort))/sort | solution.py:16
  10.2 146.4 %all-gather.8.cloned.1.call-start = ((), (), s32[]{:S(2)}) async-start(), calls=%async_computation.5 | async-start | bytes 5570560 | tf_op jit(solution)/shard_map/all_gather | solution.py:87
  18.8 8.8 %copy-start.3 = (f32[2,4096]{1,0:T(2,128)S(1)}, f32[2,4096]{1,0:T(2,128)}, u32[]{:S(2)}) copy-start(f32[2,4096]{1,0:T(2,128)} %param.8) | copy-start | bytes 98308
  18.8 8.8 %copy-start.4 = (f32[2,2,128]{2,1,0:T(2,128)S(1)}, f32[2,2,128]{2,1,0:T(2,128)}, u32[]{:S(2)}) copy-start(f32[2,2,128]{2,1,0:T(2,128)} %param.10) | copy-start | bytes 6148
  102.6 3.3 %slice-start = ((s8[6291456]{0:T(1024)(128)(4,1)}), s8[4194304]{0:T(1024)(128)(4,1)S(1)}, s32[]{:S(2)}) async-start(s8[6291456]{0:T(1024)(128)(4,1)} %bitcast.82), calls=%async_computation.9 | async-start | bytes 8388608
  103.7 2.1 slice-start.1
  105.8 7.4 %copy-start.2 = (s32[16,512]{1,0:T(8,128)S(1)}, s32[16,512]{1,0:T(8,128)}, u32[]{:S(2)}) copy-start(s32[16,512]{1,0:T(8,128)} %reshape.304) | copy-start | bytes 98308
  110.9 1.3 copy-start.1
  113.2 87.7 %all-gather.6.cloned.1.call-start = ((), (), s32[]{:S(2)}) async-start(), calls=%async_computation.4 | async-start | bytes 5570560 | tf_op jit(solution)/shard_map/all_gather | solution.py:88
  116.9 191.6 %reduce-scatter.2.cloned.1.call-start = ((), (), s32[]{:S(2)}) async-start(), calls=%async_computation.6 | async-start | bytes 5570560 | tf_op jit(solution)/shard_map/reduce_scatter | solution.py:116
Sparse Core Ops, SparseCore 0:
  10.6 65.4 all-gather.3
  113.3 43.1 all-gather.7
  158.3 42.5 all-gather.5
  227.5 80.8 reduce-scatter.1
Sparse Core Ops, SparseCore 1:
  11.0 2.4 sort.39.cloned.1.call-done
  (1 shorter events, 0.0 us)
where the time goes:
time: 326 us; the launch traced here: 325 us
  waiting for transfers between devices  145 us (44%)
  local copies, waits for them, and re-layouts  66.6 us (20%)
  matrix products  57.9 us (18%)
  other arithmetic  21.1 us (6%)
  between operations  17.4 us (5%)
  blocking collectives  15.6 us (5%)
    reduce_scatter x1, waiting for transfers between devices, body(): lax.psum_scatter(head_terms.astype(jnp.bfloat16), 'tp', scatter_dimension...  77.9 us
    all_gather x1, waiting for transfers between devices, body(): gathered = lax.all_gather(tokens, 'tp', axis=1, tiled=True)  48.4 us
    gather x64, local copies, waits for them, and re-layouts  30.5 us
    dot_general x1, matrix products, body(): jnp.einsum('rhe,khe->hrk', query_rows, key_piece.reshape(count, heads_her...  26.4 us
    dot_general x1, matrix products, body(): jnp.einsum('hrk,khe->rhe', rounded, value_piece.reshape(count, heads_here...  22.6 us
    all_gather x1, waiting for transfers between devices, body(): value_piece = lax.all_gather(value_rows, ('mod', 'seq'), axis=0, tiled=True)  18 us
    gather x1, local copies, waits for them, and re-layouts, select_rows(): table[picked]  14.3 us
    unnamed x18, local copies, waits for them, and re-layouts  10.2 us
  transfers between devices with their start and end apart: 4, of which 4 were waited for; matrix products, arithmetic and copies ran while one was open for 27% of the time, Pallas kernels for 0%

commit v1 on v0

--- a/solution.py
+++ b/solution.py
@@ -9,6 +9,12 @@
 CAP = 320
 epsilon = 1e-05
 sentinel = 1 << 30
+
+
+def gather_from_all(x, axis, dim):
+    devices = lax.axis_size(axis)
+    repeats = [devices if d == dim else 1 for d in range(x.ndim)]
+    return lax.all_to_all(jnp.tile(x, repeats), axis, split_axis=dim, concat_axis=dim, tiled=True)
 
 
 def route_table(shard_ids, shard_index, slot_count):
@@ -60,7 +66,7 @@
     )
     key_grid = tables[5].reshape(mod_count, seq_count, 2, CAP)
     key_order = jnp.transpose(key_grid, (2, 1, 0, 3)).reshape(shards * mod_count * CAP)
-    gathered = lax.all_gather(tokens, "tp", axis=1, tiled=True)
+    gathered = gather_from_all(tokens, "tp", 1)
     arrived = lax.all_to_all(
         select_rows(gathered, picked, live), "mod", split_axis=0, concat_axis=0, tiled=True
     )

time: 326 us -> 343 us (1.052)
  starting transfers between devices: 0.35 us -> 8.12 us
  local copies, waits for them, and re-layouts: 66.6 us -> 74.2 us
    all_gather x1 -> x0, waiting for transfers between devices: 48.4 us -> none  [body(): gathered = lax.all_gather(tokens, 'tp', axis=1, tiled=True)]
    all_to_all x0 -> x1, waiting for transfers between devices: none -> 42.6 us  [gather_from_all(): lax.all_to_all(jnp.tile(x, repeats), axis, split_axis=dim, concat_axis=di...]
    all_to_all x0 -> x1, starting transfers between devices: none -> 7.77 us  [gather_from_all(): lax.all_to_all(jnp.tile(x, repeats), axis, split_axis=dim, concat_axis=di...]
    all_gather x1, waiting for transfers between devices: 0.12 us -> 7.35 us  [body(): key_piece = lax.all_gather(key_rows, ('mod', 'seq'), axis=0, tiled=True)]
    all_to_all x0 -> x1, local copies, waits for them, and re-layouts: none -> 4.79 us  [gather_from_all(): lax.all_to_all(jnp.tile(x, repeats), axis, split_axis=dim, concat_axis=di...]
    another operation x0 -> x1, local copies, waits for them, and re-layouts: none -> 3.58 us  [gather_from_all(): jnp.tile(x, repeats)]
    unnamed x18 -> x20, local copies, waits for them, and re-layouts: 10.2 us -> 10.2 us
  transfers between devices with their start and end apart: 4 -> 4, of which waited for: 4 -> 4; matrix products, arithmetic and copies ran while one was open for 27% -> 26% of each run, Pallas kernels for 0% -> 0%
where the time goes in v1:
time: 343 us; the launch traced here: 341 us
  waiting for transfers between devices  145 us (42%)
  local copies, waits for them, and re-layouts  74.2 us (22%)
  matrix products  57.9 us (17%)
  other arithmetic  21.1 us (6%)
  between operations  17.7 us (5%)
  blocking collectives  16.5 us (5%)
  starting transfers between devices  8.12 us (2%)
    reduce_scatter x1, waiting for transfers between devices, body(): lax.psum_scatter(head_terms.astype(jnp.bfloat16), 'tp', scatter_dimension...  77.7 us
    all_to_all x1, waiting for transfers between devices, gather_from_all(): lax.all_to_all(jnp.tile(x, repeats), axis, split_axis=dim, concat_axis=di...  42.6 us
    gather x64, local copies, waits for them, and re-layouts  30.5 us
    dot_general x1, matrix products, body(): jnp.einsum('rhe,khe->hrk', query_rows, key_piece.reshape(count, heads_her...  26.4 us
    dot_general x1, matrix products, body(): jnp.einsum('hrk,khe->rhe', rounded, value_piece.reshape(count, heads_here...  22.6 us
    all_gather x1, waiting for transfers between devices, body(): value_piece = lax.all_gather(value_rows, ('mod', 'seq'), axis=0, tiled=True)  17.7 us
    gather x1, local copies, waits for them, and re-layouts, select_rows(): table[picked]  14.3 us
    unnamed x20, local copies, waits for them, and re-layouts  10.2 us
  transfers between devices with their start and end apart: 4, of which 4 were waited for; matrix products, arithmetic and copies ran while one was open for 26% of the time, Pallas kernels for 0%

profile of v1, /device:TPU:1, one launch (start us, length us, event | category | flops | bytes accessed | tf_op | source)
XLA Modules:
  0.0 341.3 jit_solution(4793576755810268711)
XLA Ops:
  7.4 3.6 %tile.2 = bf16[512,16,256]{2,0,1:T(8,128)(2,1)} broadcast(bf16[512,256]{1,0:T(8,128)(2,1)} %param.6), dimensions={0,2} | broadcast | bytes 4456448 | tf_op jit(solution)/shard_map/tile | solution.py:17
  11.0 7.8 %all-to-all-start = ((bf16[512,16,256]{2,0,1:T(8,128)(2,1)}), bf16[512,16,256]{2,0,1:T(8,128)(2,1)}, u32[]{:S(2)}, u32[]{:S(2)}) async-start(bf16[512,16,256]{2,0,1:T(8,128)(2,1)} %tile.2), calls=%async_computation | async-start | bytes 8388608 | tf_op jit(solution)/shard_map/all_to_all | solution.py:17
  22.8 3.8 %sort.34 = (s32[512]{0:T(512)}, s32[512]{0:T(512)S(1)}) sort(s32[512]{0:T(512)S(1)} %bitcast.95, s32[512]{0:T(512)S(1)} %iota.35), dimensions={0}, to_apply=%region_1.2 | sort | flops 4608 | bytes 8192 | tf_op jit(solution)/shard_map/jit(argsort)/sort | solution.py:22
  28.1 8.8 %copy.18 = bf16[1,4096,3,256]{1,3,2,0:T(8,128)(2,1)} copy(bf16[1,4096,3,256]{3,1,2,0:T(8,128)(2,1)} %param.9) | data formatting | bytes 12582912 | tf_op args[3]
  37.6 42.6 %all-to-all-done = bf16[512,16,256]{2,0,1:T(8,128)(2,1)} async-done(((bf16[512,16,256]{2,0,1:T(8,128)(2,1)}), bf16[512,16,256]{2,0,1:T(8,128)(2,1)}, u32[]{:S(2)}, u32[]{:S(2)}) %all-to-all-start) | async-done | bytes 4194336 | tf_op jit(solution)/shard_map/all_to_all | solution.py:17
  80.2 4.8 %copy.25 = bf16[16,64,8,256]{3,2,0,1:T(8,128)(2,1)} copy(bf16[16,64,8,256]{3,2,1,0:T(8,128)(2,1)} %bitcast.40) | data formatting | bytes 8388608 | tf_op jit(solution)/shard_map/all_to_all | solution.py:17
  85.0 14.3 %gather_fusion = bf16[640,4096]{1,0:T(8,128)(2,1)} fusion(bf16[512,4096]{1,0:T(8,128)(2,1)} %bitcast.82, s32[1024]{0:T(1024)S(1)} %pad_clamp_fusion.1), kind=kCustom, calls=%fused_computation | custom fusion | bytes 10488320 | tf_op jit(solution)/shard_map/gather | solution.py:37
  99.4 2.9 broadcast_select_fusion
  102.3 10.0 %all_to_all.19 = bf16[2,320,4096]{2,1,0:T(8,128)(2,1)S(1)} all-to-all(bf16[2,320,4096]{2,1,0:T(8,128)(2,1)S(1)} %broadcast_select_fusion), channel_id=1, replica_groups=mesh['mod'=2,'seq'=8,'tp'=16] {'mod'}, dimensions={0} | all-to-all | bytes 10485760 | tf_op jit(solution)/shard_map/all_to_all | solution.py:70
  113.4 2.1 fusion.7
  115.6 5.1 %fusion.29 = f32[640,3,2,128]{0,3,2,1:T(8,128)S(1)} fusion(bf16[640,4096,1,1]{1,0,3,2:T(8,128)(2,1)S(1)} %bitcast.88, bf16[3,2,128,4096]{3,2,1,0:T(8,128)(2,1)S(1)} %bitcast.87), kind=kOutput, calls=%fused_computation.75 | convolution fusion | flops 4026531840 | bytes 13500416 | tf_op jit(solution)/shard_map/dot_general | solution.py:82
  120.7 1.3 copy-done.1
  124.8 1.8 slice.59
  126.9 30.9 %while.1 = (s32[]{:T(128)}, s32[16,832]{1,0:T(8,128)S(1)}, s32[16,2]{0,1:T(2,128)S(1)}, s32[16,320]{1,0:T(8,128)S(1)}, s32[]{:T(128)}, /*index=5*/s32[]{:T(128)}) while((s32[]{:T(128)}, s32[16,832]{1,0:T(8,128)S(1)}, s32[16,2]{0,1:T(2,128)S(1)}, s32[16,320]{1,0:T(8,128)S(1)}, s32[]{:T(128)}, /*index=5*/s32[]{:T(128)}) %tuple.26), condition=%wide.while_cond, body=%wide.while_body.sunk | while | flops 2 | bytes 5233 | solution.py:27
  158.1 6.8 %broadcast_compare_fusion = pred[640,10240]{1,0:T(8,128)(4,1)} fusion(s32[10240]{0:T(1024)S(1)} %le.22, s32[640]{0:T(1024)S(1)} %le.24), kind=kLoop, calls=%fused_computation.9 | loop fusion | flops 6553600 | bytes 6597120 | tf_op jit(solution)/shard_map/le | solution.py:105
  166.1 7.3 %all-gather.5.cloned.1.call-done = bf16[10240,256]{0,1:T(8,128)(2,1)} async-done(((bf16[640,256]{0,1:T(8,128)(2,1)}), bf16[10240,256]{0,1:T(8,128)(2,1)}) %all-gather.5.cloned.1.call-update) | async-done | bytes 5242896 | tf_op jit(solution)/shard_map/all_gather | solution.py:93
  173.5 26.4 %fusion = (f32[2,640]{1,0:T(2,128)S(1)}, f32[2,640,10240]{2,1,0:T(8,128)}) fusion(pred[640,10240]{1,0:T(8,128)(4,1)} %broadcast_compare_fusion, bf16[10240,2,128]{0,2,1:T(8,128)(2,1)} %bitcast.98, f32[640,3,2,128]{0,3,2,1:T(8,128)} %copy-done.1, f32[128]{0:T(128)S(1)} %get-tuple-element.33, f32[640,2]{0,1:T(2,128)S(1)} %add_rsqrt_fusion.1), kind=kOutput, calls=%fused_computation.5 | convolution fusion | flops 3395255040 | bytes 64891392 | tf_op jit(solution)/shard_map/rhe,khe->hrk/dot_general | solution.py:97
  199.9 17.7 %all-gather.3.cloned.1.call-done = bf16[10240,256]{0,1:T(8,128)(2,1)} async-done(((bf16[640,256]{0,1:T(8,128)(2,1)}), bf16[10240,256]{0,1:T(8,128)(2,1)}) %all-gather.3.cloned.1.call-update) | async-done | bytes 5242896 | tf_op jit(solution)/shard_map/all_gather | solution.py:94
  217.6 22.6 %fusion.15 = bf16[640,2,128]{0,2,1:T(8,128)(2,1)S(1)} fusion(bf16[10240,2,128]{0,2,1:T(8,128)(2,1)} %bitcast.99, f32[2,640,10240]{2,1,0:T(8,128)} %get-tuple-element.36, pred[640,10240]{1,0:T(8,128)(4,1)} %broadcast_compare_fusion, f32[640,2]{0,1:T(2,128)S(1)} %select_bitcast_fusion.2), kind=kOutput, calls=%fused_computation.20 | convolution fusion | flops 3395092480 | bytes 64558080 | tf_op jit(solution)/shard_map/hrk,khe->rhe/dot_general | solution.py:108
  240.2 3.9 %convolution_convert_fusion = bf16[640,4096]{1,0:T(8,128)(2,1)} fusion(bf16[640,256]{0,1:T(8,128)(2,1)S(1)} %bitcast.90, bf16[1,256,4096]{2,1,0:T(8,128)(2,1)S(1)} %copy-done), kind=kOutput, calls=%fused_computation.15 | convolution fusion | flops 1344798720 | bytes 7667712 | tf_op jit(solution)/shard_map/dot_general | solution.py:121
  244.1 2.4 scatter_custom_fusion
  247.2 77.7 %reduce-scatter.2.cloned.1.call-done = bf16[640,256]{1,0:T(8,128)(2,1)} async-done(((bf16[640,4096]{1,0:T(8,128)(2,1)}), bf16[640,256]{1,0:T(8,128)(2,1)}) %reduce-scatter.2.cloned.1.call-update) | async-done | bytes 327696 | tf_op jit(solution)/shard_map/reduce_scatter | solution.py:122
  324.9 6.4 %all_to_all.20 = bf16[2,320,256]{2,1,0:T(8,128)(2,1)S(1)} all-to-all(bf16[2,320,256]{2,1,0:T(8,128)(2,1)} %bitcast.91), channel_id=1, replica_groups=mesh['mod'=2,'seq'=8,'tp'=16] {'mod'}, dimensions={0} | all-to-all | bytes 655360 | tf_op jit(solution)/shard_map/all_to_all | solution.py:126
  331.3 2.6 gather_fusion.1
  (134 shorter events, 40.4 us)
Async XLA Ops:
  7.4 232.8 %copy-start = (bf16[1,256,4096]{2,1,0:T(8,128)(2,1)S(1)}, bf16[1,256,4096]{2,1,0:T(8,128)(2,1)}, u32[]{:S(2)}) copy-start(bf16[1,256,4096]{2,1,0:T(8,128)(2,1)} %param.11) | copy-start | bytes 6291460
  11.0 7.8 %copy-start.3 = (s32[8192]{0:T(1024)S(1)}, s32[8192]{0:T(1024)}, u32[]{:S(2)}) copy-start(s32[8192]{0:T(1024)} %param.7) | copy-start | bytes 98308
  11.0 69.3 %all-to-all-start = ((bf16[512,16,256]{2,0,1:T(8,128)(2,1)}), bf16[512,16,256]{2,0,1:T(8,128)(2,1)}, u32[]{:S(2)}, u32[]{:S(2)}) async-start(bf16[512,16,256]{2,0,1:T(8,128)(2,1)} %tile.2), calls=%async_computation | async-start | bytes 8388608 | tf_op jit(solution)/shard_map/all_to_all | solution.py:17
  18.7 104.5 %sort.37.cloned.1.call-start = ((), (), s32[]{:S(2)}) async-start(), calls=%async_computation.7 | async-start | bytes 196640 | tf_op jit(solution)/shard_map/vmap(jit(argsort))/sort | solution.py:22
  20.0 153.4 %all-gather.5.cloned.1.call-start = ((), (), s32[]{:S(2)}) async-start(), calls=%async_computation.5 | async-start | bytes 5570560 | tf_op jit(solution)/shard_map/all_gather | solution.py:93
  28.0 8.8 %copy-start.5 = (f32[2,2,128]{2,1,0:T(2,128)S(1)}, f32[2,2,128]{2,1,0:T(2,128)}, u32[]{:S(2)}) copy-start(f32[2,2,128]{2,1,0:T(2,128)} %param.10) | copy-start | bytes 6148
  28.0 9.5 %copy-start.4 = (f32[2,4096]{1,0:T(2,128)S(1)}, f32[2,4096]{1,0:T(2,128)}, u32[]{:S(2)}) copy-start(f32[2,4096]{1,0:T(2,128)} %param.8) | copy-start | bytes 98308
  112.3 3.3 slice-start
  113.4 2.1 slice-start.1
  115.6 7.4 %copy-start.2 = (s32[16,512]{1,0:T(8,128)S(1)}, s32[16,512]{1,0:T(8,128)}, u32[]{:S(2)}) copy-start(s32[16,512]{1,0:T(8,128)} %reshape.311) | copy-start | bytes 98308
  120.6 1.3 copy-start.1
  122.9 94.7 %all-gather.3.cloned.1.call-start = ((), (), s32[]{:S(2)}) async-start(), calls=%async_computation.4 | async-start | bytes 5570560 | tf_op jit(solution)/shard_map/all_gather | solution.py:94
  126.6 198.3 %reduce-scatter.2.cloned.1.call-start = ((), (), s32[]{:S(2)}) async-start(), calls=%async_computation.6 | async-start | bytes 5570560 | tf_op jit(solution)/shard_map/reduce_scatter | solution.py:122
Sparse Core Ops, SparseCore 0:
  22.0 2.4 sort.39.cloned.1.call-done
  244.2 80.6 reduce-scatter.1
  (1 shorter events, 0.0 us)
Sparse Core Ops, SparseCore 1:
  123.0 50.4 all-gather.4
  175.1 42.4 all-gather.2
